TPU v7x, 32 devices: a whole 2x2x4 slice. The times are simulated.
32 devices in a mesh: groups: 2 (over y), row: 4 (over x, core), col: 4 (over z).
Axes of the slice: x: 2, y: 2, z: 4, core: 2. Of those that a mesh axis runs over, the one named last changes fastest.
Arguments:
- slope_matrix: bfloat16 [1024, 1024], P(('groups', 'row'), 'col'), parts along dimension 0, may hold values from -0.3125 to 0.3125
- prior_matrix: bfloat16 [1024, 1024], P(('groups', 'row'), 'col'), parts along dimension 0, may hold values from -0.3125 to 0.3125
- slope_blocks: int32 [8, 8], P(('groups', 'row'), 'col'), parts along dimension 0, may hold values from 0 to 23, as said below
- prior_blocks: int32 [8, 8], P(('groups', 'row'), 'col'), parts along dimension 0, may hold values from 0 to 23, as said below
- weight_ids: int32 [512], P(('groups', 'row')), parts along dimension 0, may hold values from 0 to 15
- valid_mask: int32 [512], P(('groups', 'row')), parts along dimension 0, may hold values 0 or 1
- noise_weights: float32 [32], P('groups'), parts along dimension 0, may hold values from 0.25 to 4
- prior_weights: bfloat16 [1024], P(('groups', 'row')), parts along dimension 0, may hold values from 0.19921875 to 2
- frames: float32 [6144, 64], P(('groups', 'row', 'col')), parts along dimension 0, may hold values from -6 to 6
Outputs:
- gram_matrix: float32 [6144, 3072], P(('groups', 'row'), 'col'), parts along dimension 0
- applied: float32 [6144, 64], P(('groups', 'row', 'col')), parts along dimension 0
There are 2 independent parts, one for each index of `groups`. A program takes and returns all parts, laid end to end along the dimension named above; each array names one. Nothing has to cross between parts.
Inputs may be any that keep to these rules, and one draw needn't show every extreme that they name: `slope_blocks`: row i names, for each block-column set c (entries c * 2 to c * 2 + 1), 2 distinct actuator blocks of that set, c * 6 to c * 6 + 5, in the order in which their blocks are stored. `prior_blocks`: row i names, for each block-column set c (entries c * 2 to c * 2 + 1), 2 distinct actuator blocks of that set, c * 6 to c * 6 + 5, in the order in which their blocks are stored.
All inputs are finite; a program needn't handle non-finite values. No bound on the sum of `valid_mask` on one device may be relied on, other than what follows from the above.
Results may differ from a plain program's by a relative error of at most 0.007.
Values may be sent and summed in bfloat16 or wider, within the bound.
No kernel may reach another device: no remote copies, remote signals or barrier semaphores. Data moves between devices by JAX's collectives and lax.ppermute only.
A program may use at most 128 MiB of HBM per device.

v0:
```python
import jax
import jax.numpy as jnp
from jax import lax
from jax.sharding import PartitionSpec as P

BS = 128
AB = 6


def from_root(block, axis, owner):
    block = jnp.where(lax.axis_index(axis) == owner, block, jnp.zeros_like(block))
    return lax.psum(block, axis)


def expand_blocks(values, block_ids, set_index):
    block_count = block_ids.shape[0]
    chosen = block_ids.shape[1]
    targets = set_index * AB + jnp.arange(AB, dtype=jnp.int32)
    onehot = (block_ids[:, :, None] == targets[None, None, :]).astype(jnp.bfloat16)
    shaped = values.reshape(block_count, BS, chosen, BS)
    expanded = jnp.einsum("rskb,rka->rsab", shaped, onehot, preferred_element_type=jnp.float32)
    return expanded.astype(jnp.bfloat16).reshape(block_count * BS, AB * BS)


def shards(
    slope_matrix,
    prior_matrix,
    slope_blocks,
    prior_blocks,
    weight_ids,
    valid_mask,
    noise_weights,
    prior_weights,
    frames,
):
    row_index = lax.axis_index("row")
    col_index = lax.axis_index("col")
    classes = jnp.arange(noise_weights.shape[0], dtype=jnp.int32)
    picked = jnp.sum(
        jnp.where(weight_ids[:, None] == classes[None, :], noise_weights[None, :], 0.0), axis=1
    )
    subap_weight = picked * valid_mask.astype(jnp.float32)
    slope_weight = jnp.repeat(subap_weight, 2).astype(jnp.bfloat16)
    local_rows = jnp.concatenate([slope_matrix, prior_matrix], axis=0)
    local_ids = jnp.concatenate([slope_blocks, prior_blocks], axis=0)
    local_weight = jnp.concatenate([slope_weight, prior_weights], axis=0)
    all_rows, all_ids, all_weight = (
        lax.all_gather(local_rows, "row", axis=0, tiled=True),
        lax.all_gather(local_ids, "row", axis=0, tiled=True),
        lax.all_gather(local_weight, "row", axis=0, tiled=True),
    )
    row_scale = all_weight.astype(jnp.float32)[:, None]
    weighted_rows = (all_rows.astype(jnp.float32) * row_scale).astype(jnp.bfloat16)
    weighted_cols = expand_blocks(weighted_rows, all_ids, col_index)
    sent_rows, sent_ids = (
        from_root(all_rows, "col", row_index),
        from_root(all_ids, "col", row_index),
    )
    row_dense = expand_blocks(sent_rows, sent_ids, row_index)
    gram_tile = lax.dot_general(
        row_dense, weighted_cols, (((0,), (0,)), ((), ())), preferred_element_type=jnp.float32
    )
    frames_rows = lax.all_gather(frames, "col", axis=0, tiled=True)
    frames_cols = from_root(frames_rows, "row", col_index)
    partial_image = jnp.dot(
        gram_tile, frames_cols, precision=lax.Precision.HIGHEST, preferred_element_type=jnp.float32
    )
    applied = lax.psum_scatter(partial_image, "col", scatter_dimension=0, tiled=True)
    return (gram_tile, applied)


def solution(mesh):
    in_specs = (
        P(("groups", "row"), "col"),
        P(("groups", "row"), "col"),
        P(("groups", "row"), "col"),
        P(("groups", "row"), "col"),
        P(("groups", "row")),
        P(("groups", "row")),
        P("groups"),
        P(("groups", "row")),
        P(("groups", "row", "col"), None),
    )
    out_specs = (P(("groups", "row"), "col"), P(("groups", "row", "col"), None))
    return jax.shard_map(shards, mesh=mesh, in_specs=in_specs, out_specs=out_specs, check_vma=False)
```

profile of v0, /device:TPU:0, one launch (start us, length us, event | category | flops | bytes accessed | tf_op | source)
XLA Modules:
  0.0 126.3 jit_solution(12584636910592303553)
XLA Ops:
  7.2 0.9 pad_maximum_fusion
  8.1 8.6 %all_gather.13 = bf16[1024,256]{1,0:T(8,128)(2,1)S(1)} all-gather(bf16[256,256]{1,0:T(8,128)(2,1)S(1)} %pad_maximum_fusion), channel_id=1, replica_groups=mesh['groups'=2,'row'=4,'col'=4] {'row'}, dimensions={0}, use_global_device_ids=true | all-gather | bytes 655360 | tf_op jit(solution)/shard_map/all_gather | solution.py:48
  16.8 0.9 reshape.31
  17.8 16.0 %all-gather.2 = f32[4,192,64]{1,2,0:T(8,128)S(1)} all-gather(f32[1,192,64]{1,2,0:T(8,128)S(1)} %bitcast.36), channel_id=1, replica_groups=mesh['groups'=2,'row'=4,'col'=4] {'col'}, dimensions={0}, use_global_device_ids=true | all-gather | bytes 245760 | tf_op jit(solution)/shard_map/all_gather | solution.py:63
  33.9 0.2 copy.31
  34.0 0.9 reshape.44
  35.0 5.1 %all-gather = s32[4,2,2]{2,1,0:T(2,128)S(1)} all-gather(s32[1,2,2]{2,1,0:T(2,128)S(1)} %add_bitcast_fusion), channel_id=1, replica_groups=mesh['groups'=2,'row'=4,'col'=4] {'row'}, dimensions={0}, use_global_device_ids=true | all-gather | bytes 80 | tf_op jit(solution)/shard_map/all_gather | solution.py:49
  40.1 0.1 copy.34
  40.2 7.8 %psum.21 = s32[8,2]{0,1:T(2,128)S(1)} all-reduce(s32[8,2]{0,1:T(2,128)S(1)} %broadcast_select_fusion.2), channel_id=1, replica_groups=mesh['groups'=2,'row'=4,'col'=4] {'col'}, use_global_device_ids=true, to_apply=%region_0.1 | all-reduce | flops 16 | bytes 128 | tf_op jit(solution)/shard_map/psum | solution.py:12
  47.9 0.1 copy.27
  48.1 0.1 select_reduce_fusion
  48.2 0.1 broadcast_in_dim.32
  48.2 0.2 convert_element_type.38
  48.4 5.1 %all-gather.1 = bf16[4,1,256]{2,1,0:T(2,128)(2,1)S(1)} all-gather(bf16[1,1,256]{2,1,0:T(2,128)(2,1)S(1)} %reshape.37), channel_id=1, replica_groups=mesh['groups'=2,'row'=4,'col'=4] {'row'}, dimensions={0}, use_global_device_ids=true | all-gather | bytes 2560 | tf_op jit(solution)/shard_map/all_gather | solution.py:50
  53.5 0.2 multiply_convert_fusion
  53.7 0.1 reshape.33
  53.8 2.2 %convolution_convert_fusion = bf16[8,6,128,128]{3,1,2,0:T(8,128)(2,1)} fusion(bf16[8,128,2,128]{3,2,1,0:T(2,128)(2,1)S(1)} %reshape.33, s32[6]{0:T(128)S(1)} %iota_add_fusion, s32[8,2]{1,0:T(8,128)S(1)} %bitcast.38), kind=kOutput, calls=%fused_computation | convolution fusion | flops 3932256 | bytes 2097240 | tf_op jit(solution)/shard_map/rskb,rka->rsab/dot_general | solution.py:21
  56.0 3.4 %all-reduce.3.cloned.1.call-done = bf16[8,128,2,128]{3,2,1,0:T(2,128)(2,1)} async-done(((bf16[8,128,2,128]{3,2,1,0:T(2,128)(2,1)}), bf16[8,128,2,128]{3,2,1,0:T(2,128)(2,1)}) %all-reduce.3.cloned.1.call-update) | async-done | bytes 524304 | tf_op jit(solution)/shard_map/psum | solution.py:12
  59.4 2.1 %convolution_convert_fusion.1 = bf16[8,6,128,128]{3,1,2,0:T(8,128)(2,1)S(1)} fusion(bf16[8,128,2,128]{3,2,1,0:T(2,128)(2,1)} %all-reduce.3.cloned.1.call-done, s32[6]{0:T(128)S(1)} %iota_add_fusion.1, s32[8,2]{1,0:T(8,128)S(1)} %copy.27), kind=kOutput, calls=%fused_computation.1 | convolution fusion | flops 3932256 | bytes 2097240 | tf_op jit(solution)/shard_map/rskb,rka->rsab/dot_general | solution.py:21
  61.5 1.5 %fusion = f32[768,768]{1,0:T(8,128)S(1)} fusion(bf16[128,8,6,128]{3,2,1,0:T(8,128)(2,1)S(1)} %bitcast.34, bf16[128,8,6,128]{3,2,1,0:T(8,128)(2,1)S(1)} %bitcast.35), kind=kOutput, calls=%fused_computation.2 | convolution fusion | flops 1207959552 | bytes 5505024 | tf_op jit(solution)/shard_map/dot_general | solution.py:60
  63.0 30.5 %all-reduce.5.cloned.1.call-done = f32[768,64]{0,1:T(8,128)} async-done(((f32[768,64]{0,1:T(8,128)}), f32[768,64]{0,1:T(8,128)}) %all-reduce.5.cloned.1.call-update) | async-done | bytes 196624 | tf_op jit(solution)/shard_map/psum | solution.py:12
  93.5 3.7 %fusion.13 = f32[768,64]{1,0:T(8,128)} fusion(f32[768,768]{1,0:T(8,128)S(1)} %fusion, f32[768,64]{0,1:T(8,128)} %all-reduce.5.cloned.1.call-done), kind=kOutput, calls=%fused_computation.27 | convolution fusion | flops 452984832 | bytes 2752512
  97.2 21.0 %reduce-scatter.4.cloned.1.call-done = f32[192,64]{1,0:T(8,128)} async-done(((f32[768,64]{1,0:T(8,128)}), f32[192,64]{1,0:T(8,128)}) %reduce-scatter.4.cloned.1.call-update) | async-done | bytes 49168
  118.2 1.6 %copy.38 = f32[192,64]{0,1:T(8,128)} copy(f32[192,64]{1,0:T(8,128)} %reduce-scatter.4.cloned.1.call-done) | data formatting | bytes 98304
  (34 shorter events, 0.3 us)
Async XLA Ops:
  7.2 10.7 %copy-start.2 = (f32[192,64]{0,1:T(8,128)S(1)}, f32[192,64]{0,1:T(8,128)}, u32[]{:S(2)}) copy-start(f32[192,64]{0,1:T(8,128)} %param.17) | copy-start | bytes 147460
  7.2 52.2 %all-reduce.3.cloned.1.call-start = ((), (), s32[]{:S(2)}) async-start(), calls=%async_computation.1 | async-start | bytes 1048576 | tf_op jit(solution)/shard_map/psum | solution.py:12
  16.8 18.2 %copy-start.3 = (s32[1,2]{1,0:T(1,128)S(1)}, s32[1,2]{1,0:T(1,128)}, u32[]{:S(2)}) copy-start(s32[1,2]{1,0:T(1,128)} %param.12) | copy-start | bytes 28
  16.8 18.2 %copy-start.4 = (s32[1,2]{1,0:T(1,128)S(1)}, s32[1,2]{1,0:T(1,128)}, u32[]{:S(2)}) copy-start(s32[1,2]{1,0:T(1,128)} %param.11) | copy-start | bytes 28
  16.8 31.3 %copy-start.5 = (f32[16]{0:T(128)S(1)}, f32[16]{0:T(128)}, u32[]{:S(2)}) copy-start(f32[16]{0:T(128)} %param.15) | copy-start | bytes 196
  16.8 31.3 %copy-start.6 = (s32[64]{0:T(128)S(1)}, s32[64]{0:T(128)}, u32[]{:S(2)}) copy-start(s32[64]{0:T(128)} %param.13) | copy-start | bytes 772
  16.8 31.4 %copy-start.7 = (s32[64]{0:T(128)S(1)}, s32[64]{0:T(128)}, u32[]{:S(2)}) copy-start(s32[64]{0:T(128)} %param.14) | copy-start | bytes 772
  16.8 31.6 %copy-start.8 = (bf16[128]{0:T(256)(128)(2,1)S(1)}, bf16[128]{0:T(256)(128)(2,1)}, u32[]{:S(2)}) copy-start(bf16[128]{0:T(256)(128)(2,1)} %param.16) | copy-start | bytes 772
  17.8 75.8 %all-reduce.5.cloned.1.call-start = ((), (), s32[]{:S(2)}) async-start(), calls=%async_computation.2 | async-start | bytes 393216 | tf_op jit(solution)/shard_map/psum | solution.py:12
  34.9 83.3 %reduce-scatter.4.cloned.1.call-start = ((), (), s32[]{:S(2)}) async-start(), calls=%async_computation.3 | async-start | bytes 491520
  59.4 2.1 %copy-start.1 = (bf16[8,6,128,128]{3,1,2,0:T(8,128)(2,1)S(1)}, bf16[8,6,128,128]{3,1,2,0:T(8,128)(2,1)}, u32[]{:S(2)}) copy-start(bf16[8,6,128,128]{3,1,2,0:T(8,128)(2,1)} %convolution_convert_fusion) | copy-start | bytes 4718596
  63.0 56.8 %copy-start = (f32[768,768]{1,0:T(8,128)}, f32[768,768]{1,0:T(8,128)S(1)}, u32[]{:S(2)}) copy-start(f32[768,768]{1,0:T(8,128)S(1)} %fusion) | copy-start | bytes 7077892
Sparse Core Ops, SparseCore 0:
  17.9 41.4 all-reduce.2
  61.7 31.7 all-reduce.4
  97.3 20.8 reduce-scatter.3
where the time goes:
time: 127 us; the launch traced here: 126 us
  waiting for transfers between devices  54.9 us (43%)
  blocking collectives  42.6 us (34%)
  between operations  13.9 us (11%)
  matrix products  9.43 us (7%)
  local copies, waits for them, and re-layouts  4.09 us (3%)
  other arithmetic  1.28 us (1%)
    psum x2, waiting for transfers between devices, from_root(): return lax.psum(block, axis)  33.9 us
    unnamed x4, waiting for transfers between devices  21 us
    all_gather x1, blocking collectives, shards(): frames_rows = lax.all_gather(frames, 'col', axis=0, tiled=True)  16 us
    all_gather x1, blocking collectives, shards(): lax.all_gather(local_rows, 'row', axis=0, tiled=True)  8.65 us
    psum x1, blocking collectives, from_root(): return lax.psum(block, axis)  7.79 us
    all_gather x1, blocking collectives, shards(): lax.all_gather(local_ids, 'row', axis=0, tiled=True)  5.07 us
    all_gather x1, blocking collectives, shards(): lax.all_gather(local_weight, 'row', axis=0, tiled=True)  5.07 us
    dot_general x2, matrix products, expand_blocks(): jnp.einsum('rskb,rka->rsab', shaped, onehot, preferred_element_type=jnp.f...  4.29 us
  transfers between devices with their start and end apart: 3, of which 3 were waited for; matrix products, arithmetic and copies ran while one was open for 6% of the time, Pallas kernels for 0%

commit v1 on v0

--- a/solution.py
+++ b/solution.py
@@ -9,7 +9,7 @@
 
 def from_root(block, axis, owner):
     block = jnp.where(lax.axis_index(axis) == owner, block, jnp.zeros_like(block))
-    return lax.psum(block, axis)
+    return jnp.sum(lax.all_gather(block, axis), axis=0)
 
 
 def expand_blocks(values, block_ids, set_index):

time: 127 us -> 105 us (0.83)
  waiting for transfers between devices: 54.9 us -> 20 us
  blocking collectives: 42.6 us -> 55 us
  other arithmetic: 1.28 us -> 4.73 us
  matrix products: 9.43 us -> 7.6 us
    psum x2 -> x0, waiting for transfers between devices: 33.9 us -> none  [from_root(): return lax.psum(block, axis)]
    all_gather x0 -> x2, blocking collectives: none -> 19.7 us  [from_root(): return jnp.sum(lax.all_gather(block, axis), axis=0)]
    psum x1 -> x0, blocking collectives: 7.79 us -> none  [from_root(): return lax.psum(block, axis)]
    reduce_sum x0 -> x3, other arithmetic: none -> 2.65 us  [from_root(): return jnp.sum(lax.all_gather(block, axis), axis=0)]
    unnamed x4 -> x3, waiting for transfers between devices: 21 us -> 19.7 us
  transfers between devices with their start and end apart: 3 -> 2, of which waited for: 3 -> 2; matrix products, arithmetic and copies ran while one was open for 6% -> 4% of each run, Pallas kernels for 0% -> 0%
where the time goes in v1:
time: 105 us
  blocking collectives  55 us (52%)
  waiting for transfers between devices  20 us (19%)
  between operations  14.3 us (14%)
  matrix products  7.6 us (7%)
  other arithmetic  4.73 us (5%)
  local copies, waits for them, and re-layouts  3.37 us (3%)
    all_gather x2, blocking collectives, from_root(): return jnp.sum(lax.all_gather(block, axis), axis=0)  19.7 us
    unnamed x3, waiting for transfers between devices  19.7 us
    all_gather x1, blocking collectives, shards(): frames_rows = lax.all_gather(frames, 'col', axis=0, tiled=True)  16.3 us
    all_gather x1, blocking collectives, shards(): lax.all_gather(local_rows, 'row', axis=0, tiled=True)  8.78 us
    all_gather x1, blocking collectives, shards(): lax.all_gather(local_ids, 'row', axis=0, tiled=True)  5.07 us
    all_gather x1, blocking collectives, shards(): lax.all_gather(local_weight, 'row', axis=0, tiled=True)  5.07 us
    dot_general x2, matrix products, expand_blocks(): jnp.einsum('rskb,rka->rsab', shaped, onehot, preferred_element_type=jnp.f...  3.4 us
    unnamed x1, matrix products  2.72 us
  transfers between devices with their start and end apart: 2, of which 2 were waited for; matrix products, arithmetic and copies ran while one was open for 4% of the time, Pallas kernels for 0%

profile of v1, /device:TPU:0, one launch (start us, length us, event | category | flops | bytes accessed | tf_op | source)
XLA Modules:
  0.0 105.0 jit_solution(8541111687152717770)
XLA Ops:
  7.3 0.9 pad_maximum_fusion
  8.2 8.8 %all_gather.33 = bf16[1024,256]{1,0:T(8,128)(2,1)S(1)} all-gather(bf16[256,256]{1,0:T(8,128)(2,1)S(1)} %pad_maximum_fusion), channel_id=1, replica_groups=mesh['groups'=2,'row'=4,'col'=4] {'row'}, dimensions={0}, use_global_device_ids=true | all-gather | bytes 655360 | tf_op jit(solution)/shard_map/all_gather | solution.py:48
  17.0 0.8 broadcast_select_fusion
  17.9 5.1 %all-gather.3 = s32[4,2,2]{2,1,0:T(2,128)S(1)} all-gather(s32[1,2,2]{2,1,0:T(2,128)S(1)} %add_bitcast_fusion), channel_id=1, replica_groups=mesh['groups'=2,'row'=4,'col'=4] {'row'}, dimensions={0}, use_global_device_ids=true | all-gather | bytes 80 | tf_op jit(solution)/shard_map/all_gather | solution.py:49
  23.1 11.5 %all-gather.4 = s32[4,8,2]{1,2,0:T(2,128)S(1)} all-gather(s32[1,8,2]{1,2,0:T(2,128)S(1)} %select_bitcast_fusion), channel_id=2, replica_groups=mesh['groups'=2,'row'=4,'col'=4] {'col'}, dimensions={0}, use_global_device_ids=true | all-gather | bytes 320 | tf_op jit(solution)/shard_map/all_gather | solution.py:12
  34.8 0.2 convert_element_type.40
  35.0 5.1 %all-gather.5 = bf16[4,1,256]{2,1,0:T(2,128)(2,1)S(1)} all-gather(bf16[1,1,256]{2,1,0:T(2,128)(2,1)S(1)} %reshape.42), channel_id=1, replica_groups=mesh['groups'=2,'row'=4,'col'=4] {'row'}, dimensions={0}, use_global_device_ids=true | all-gather | bytes 2560 | tf_op jit(solution)/shard_map/all_gather | solution.py:50
  40.1 0.2 multiply_convert_fusion
  40.3 0.1 reshape.33
  40.4 16.3 %all-gather.6 = f32[4,192,64]{1,2,0:T(8,128)S(1)} all-gather(f32[1,192,64]{1,2,0:T(8,128)S(1)} %bitcast.42), channel_id=1, replica_groups=mesh['groups'=2,'row'=4,'col'=4] {'col'}, dimensions={0}, use_global_device_ids=true | all-gather | bytes 245760 | tf_op jit(solution)/shard_map/all_gather | solution.py:63
  56.8 0.2 copy.29
  56.9 0.2 reshape.49
  57.1 8.3 %all-gather.2 = f32[3072,64]{0,1:T(8,128)S(1)} all-gather(f32[768,64]{0,1:T(8,128)S(1)} %reshape.49), channel_id=4, replica_groups=mesh['groups'=2,'row'=4,'col'=4] {'row'}, dimensions={0}, use_global_device_ids=true | all-gather | bytes 983040 | tf_op jit(solution)/shard_map/all_gather | solution.py:12
  65.4 0.4 reshape.37
  65.8 0.5 reduce_sum.42
  66.3 2.2 %convolution_convert_fusion = bf16[8,6,128,128]{3,1,2,0:T(8,128)(2,1)} fusion(bf16[8,128,2,128]{3,2,1,0:T(2,128)(2,1)S(1)} %reshape.33, s32[6]{0:T(128)S(1)} %iota_add_fusion, s32[8,2]{1,0:T(8,128)S(1)} %bitcast.44), kind=kOutput, calls=%fused_computation | convolution fusion | flops 3932256 | bytes 2097240 | tf_op jit(solution)/shard_map/rskb,rka->rsab/dot_general | solution.py:21
  68.5 0.2 all-gather.9.cloned.1.call-done
  68.7 2.2 %reduce_sum.40 = bf16[1024,256]{1,0:T(8,128)(2,1)S(1)} reduce(bf16[4,1024,256]{2,1,0:T(8,128)(2,1)} %bitcast.39, bf16[]{:T(256)} %constant.16.clone.1), dimensions={0}, to_apply=%region_1.2 | reduce | flops 786432 | bytes 2621442 | tf_op jit(solution)/shard_map/reduce_sum | solution.py:12
  71.0 1.2 %convolution_convert_fusion.1 = bf16[8,6,128,128]{3,1,2,0:T(8,128)(2,1)S(1)} fusion(bf16[8,128,2,128]{3,2,1,0:T(2,128)(2,1)S(1)} %reshape.31, s32[6]{0:T(128)S(1)} %iota_add_fusion.1, s32[8,2]{1,0:T(8,128)S(1)} %copy.25), kind=kOutput, calls=%fused_computation.1 | convolution fusion | flops 3932256 | bytes 2097240 | tf_op jit(solution)/shard_map/rskb,rka->rsab/dot_general | solution.py:21
  72.3 0.4 copy-done.1
  72.6 1.5 %fusion = f32[768,768]{1,0:T(8,128)S(1)} fusion(bf16[128,8,6,128]{3,2,1,0:T(8,128)(2,1)S(1)} %bitcast.40, bf16[128,8,6,128]{3,2,1,0:T(8,128)(2,1)S(1)} %bitcast.41), kind=kOutput, calls=%fused_computation.2 | convolution fusion | flops 1207959552 | bytes 5505024 | tf_op jit(solution)/shard_map/dot_general | solution.py:60
  74.1 2.7 %fusion.13 = f32[768,64]{1,0:T(8,128)} fusion(f32[768,768]{1,0:T(8,128)S(1)} %fusion, f32[768,64]{0,1:T(8,128)S(1)} %reduce_sum.42), kind=kOutput, calls=%fused_computation.27 | convolution fusion | flops 452984832 | bytes 2752512
  76.8 19.7 %reduce-scatter.4.cloned.1.call-done = f32[192,64]{1,0:T(8,128)} async-done(((f32[768,64]{1,0:T(8,128)}), f32[192,64]{1,0:T(8,128)}) %reduce-scatter.4.cloned.1.call-update) | async-done | bytes 49168
  96.6 1.6 %copy.36 = f32[192,64]{0,1:T(8,128)} copy(f32[192,64]{1,0:T(8,128)} %reduce-scatter.4.cloned.1.call-done) | data formatting | bytes 98304
  (36 shorter events, 0.7 us)
Async XLA Ops:
  7.2 10.7 %copy-start.4 = (s32[1,2]{1,0:T(1,128)S(1)}, s32[1,2]{1,0:T(1,128)}, u32[]{:S(2)}) copy-start(s32[1,2]{1,0:T(1,128)} %param.11) | copy-start | bytes 28
  7.2 10.7 %copy-start.3 = (s32[1,2]{1,0:T(1,128)S(1)}, s32[1,2]{1,0:T(1,128)}, u32[]{:S(2)}) copy-start(s32[1,2]{1,0:T(1,128)} %param.12) | copy-start | bytes 28
  7.2 27.4 %copy-start.6 = (s32[64]{0:T(128)S(1)}, s32[64]{0:T(128)}, u32[]{:S(2)}) copy-start(s32[64]{0:T(128)} %param.13) | copy-start | bytes 772
  7.2 27.4 %copy-start.5 = (f32[16]{0:T(128)S(1)}, f32[16]{0:T(128)}, u32[]{:S(2)}) copy-start(f32[16]{0:T(128)} %param.15) | copy-start | bytes 196
  7.2 27.5 %copy-start.7 = (s32[64]{0:T(128)S(1)}, s32[64]{0:T(128)}, u32[]{:S(2)}) copy-start(s32[64]{0:T(128)} %param.14) | copy-start | bytes 772
  7.2 27.7 %copy-start.8 = (bf16[128]{0:T(256)(128)(2,1)S(1)}, bf16[128]{0:T(256)(128)(2,1)}, u32[]{:S(2)}) copy-start(bf16[128]{0:T(256)(128)(2,1)} %param.16) | copy-start | bytes 772
  7.2 61.5 %all-gather.9.cloned.1.call-start = ((), (), s32[]{:S(2)}) async-start(), calls=%async_computation.1 | async-start | bytes 2621440 | tf_op jit(solution)/shard_map/all_gather | solution.py:12
  8.2 32.3 %copy-start.2 = (f32[192,64]{0,1:T(8,128)S(1)}, f32[192,64]{0,1:T(8,128)}, u32[]{:S(2)}) copy-start(f32[192,64]{0,1:T(8,128)} %param.17) | copy-start | bytes 147460
  17.8 78.7 %reduce-scatter.4.cloned.1.call-start = ((), (), s32[]{:S(2)}) async-start(), calls=%async_computation.2 | async-start | bytes 491520
  71.0 1.6 %copy-start.1 = (bf16[8,6,128,128]{3,1,2,0:T(8,128)(2,1)S(1)}, bf16[8,6,128,128]{3,1,2,0:T(8,128)(2,1)}, u32[]{:S(2)}) copy-start(bf16[8,6,128,128]{3,1,2,0:T(8,128)(2,1)} %convolution_convert_fusion) | copy-start | bytes 4718596
  74.1 24.1 %copy-start = (f32[768,768]{1,0:T(8,128)}, f32[768,768]{1,0:T(8,128)S(1)}, u32[]{:S(2)}) copy-start(f32[768,768]{1,0:T(8,128)S(1)} %fusion) | copy-start | bytes 7077892
Sparse Core Ops, SparseCore 0:
  17.9 50.7 all-gather.8
  77.0 19.5 reduce-scatter.3
